TPU v7x, 256 devices: a whole 4x4x8 slice. The times are simulated.
256 devices in a mesh: blk: 32 (over x_lo, z, core), own: 8 (over y, x_hi).
Axes of the slice: x: 4 (x_hi: 2, x_lo: 2; x = x_hi * 2 + x_lo), y: 4, z: 8, core: 2. Of those that a mesh axis runs over, the one named last changes fastest.
Arguments:
- embeddings: bfloat16 [32768, 768], P(('blk', 'own')), may hold values from -320 to 320
- centroids: bfloat16 [16384, 768], P('blk'), may hold values from -4 to 4
- log_weight: float32 [16384], P('blk'), may hold values from -0.5 to 1.6
Outputs:
- new_centroids: float32 [16384, 768], P(('blk', 'own'))
- counts: float32 [16384], P(('blk', 'own'))
- log_norm: float32 [32768], P(('blk', 'own'))
All inputs are finite; a program needn't handle non-finite values.
Results may differ from a plain program's by a relative error of at most 0.0015.
Values may be sent and summed in bfloat16 or wider, within the bound.
No kernel may reach another device: no remote copies, remote signals or barrier semaphores. Data moves between devices by JAX's collectives and lax.ppermute only.
A program may use at most 64 MiB of HBM per device.

v0:
```python
import math
import jax
import jax.numpy as jnp
from jax import lax
from jax.sharding import PartitionSpec as P

prior_mass = 1.0


def copy_for_each(array, axis):
    copies = jnp.broadcast_to(array, (lax.axis_size(axis), *array.shape))
    return lax.all_to_all(copies, axis, split_axis=0, concat_axis=0, tiled=True)


def collected_together(array, axis):
    leaves = jax.tree.leaves(array)
    turns = sorted(range(len(leaves)), key=lambda k: -leaves[k].size)
    width = (1, *leaves[turns[0]].shape)[-1]
    lines = [
        jnp.pad(leaves[k].reshape(-1), (0, -leaves[k].size % width)).reshape(-1, width)
        for k in turns
    ]
    both, at, found = (copy_for_each(jnp.concatenate(lines), axis), 0, {})
    for k, line in zip(turns, lines):
        share = both[:, at : at + len(line)].reshape(len(both), -1)
        found[k] = share[:, : leaves[k].size].reshape(-1, *leaves[k].shape)
        at += len(line)
    numbers = iter(range(len(leaves)))
    return jax.tree.map(lambda _: found[next(numbers)], array)


def combined_pairwise(pieces, combine):
    while len(jax.tree.leaves(pieces)[0]) > 1:
        pieces = jax.vmap(combine)(
            *(jax.tree.map(lambda part: part[side::2], pieces) for side in (0, 1))
        )
    return jax.tree.map(lambda part: part[0], pieces)


def merged(array, axis, combine):
    pieces = collected_together(array, axis)
    return combined_pairwise(pieces, combine)


def cut_along(array, dim, count):
    lengths = array.shape
    tiles = array.reshape(*lengths[:dim], count, lengths[dim] // count, *lengths[dim + 1 :])
    return jnp.moveaxis(tiles, dim, 0)


def sent_and_summed(array, axis, dim):
    count = lax.axis_size(axis)
    tiles = lax.all_to_all(cut_along(array, dim, count), axis, 0, 0, tiled=True)
    return jnp.sum(tiles, axis=0)


def score_rows(row_block, centroids, half_sq, log_weight, scale_root):
    dots = lax.dot_general(
        row_block, centroids, (((1,), (1,)), ((), ())), preferred_element_type=jnp.float32
    )
    return (dots - half_sq[None, :]) / scale_root + log_weight[None, :]


def local(embeddings, centroids, log_weight):
    row_count, feat_dim = embeddings.shape
    local_count = centroids.shape[0]
    centre_vals = centroids.astype(jnp.float32)
    half_sq = 0.5 * jnp.sum(centre_vals * centre_vals, axis=1)
    scale_root = math.sqrt(feat_dim)
    logits = score_rows(
        lax.all_gather(embeddings, "blk", axis=0, tiled=True),
        centroids,
        half_sq,
        log_weight,
        scale_root,
    )
    peak_val = jnp.max(logits, axis=1)
    peak_part = peak_val
    mass_part = jnp.sum(jnp.exp(logits - peak_val[:, None]), axis=1)
    peak_val = peak_part
    mass_sum = mass_part

    def combine(first_pair, later_pair):
        joined = jnp.maximum(first_pair[0], later_pair[0])
        return (
            joined,
            first_pair[1] * jnp.exp(first_pair[0] - joined)
            + later_pair[1] * jnp.exp(later_pair[0] - joined),
        )

    peak_val, mass_sum = merged((peak_val, mass_sum), "blk", combine)
    log_total = peak_val + jnp.log(mass_sum)
    empty_sums = jnp.zeros((local_count, feat_dim), jnp.float32)
    empty_counts = jnp.zeros((local_count,), jnp.float32)
    row_block = lax.all_gather(embeddings, "blk", axis=0, tiled=True)
    logits = score_rows(row_block, centroids, half_sq, log_weight, scale_root)
    resp_vals = jnp.exp(logits - log_total[:, None])
    contrib = lax.dot_general(
        resp_vals.astype(jnp.bfloat16),
        row_block,
        (((0,), (0,)), ((), ())),
        preferred_element_type=jnp.float32,
    )
    contrib, count_part = (contrib, jnp.sum(resp_vals, axis=0))
    weighted = contrib
    counts = (empty_sums, empty_counts)[1] + count_part
    weighted, counts = (sent_and_summed(weighted, "own", 0), sent_and_summed(counts, "own", 0))
    owned_count = local_count // lax.axis_size("own")
    own_index = lax.axis_index("own")
    own_centres = lax.dynamic_slice_in_dim(centre_vals, own_index * owned_count, owned_count, 0)
    updated = (weighted + prior_mass * own_centres) / (counts[:, None] + prior_mass)
    log_norm = lax.dynamic_slice_in_dim(log_total, lax.axis_index("blk") * row_count, row_count, 0)
    return (updated, counts, log_norm)


def solution(mesh):
    placed = (P(("blk", "own"), None), P("blk", None), P("blk"))
    return jax.shard_map(
        local,
        mesh=mesh,
        in_specs=placed,
        out_specs=(P(("blk", "own"), None), P(("blk", "own")), P(("blk", "own"))),
        check_vma=False,
    )
```

profile of v0, /device:TPU:32, one launch (start us, length us, event | category | flops | bytes accessed | tf_op | source)
XLA Modules:
  0.0 191.8 jit_solution(2781830788650535467)
XLA Ops:
  7.2 0.7 all-gather.2.cloned.1.call-update
  7.9 1.4 multiply_reduce_fusion
  9.3 72.4 %all-gather.2.cloned.1.call-done = bf16[4096,768]{1,0:T(8,128)(2,1)} async-done(((bf16[128,768]{1,0:T(8,128)(2,1)}), bf16[4096,768]{1,0:T(8,128)(2,1)}) %all-gather.2.cloned.1.call-update) | async-done | bytes 6291472 | tf_op jit(solution)/shard_map/all_gather | solution.py:95
  81.6 5.9 %fusion.8 = (f32[4096]{0:T(1024)S(1)}, f32[4096,512]{0,1:T(8,128)S(1)}) fusion(f32[512]{0:T(512)} %param.5, f32[512]{0:T(512)S(1)} %broadcast_multiply_fusion, bf16[4096,768]{1,0:T(8,128)(2,1)} %all-gather.2.cloned.1.call-done, bf16[512,768]{1,0:T(8,128)(2,1)} %param.4), kind=kOutput, calls=%fused_computation.26 | convolution fusion | flops 3229609984 | bytes 15486976 | tf_op jit(solution)/shard_map/dot_general | solution.py:58
  87.5 3.2 %copy-done = f32[4096,512]{0,1:T(8,128)} copy-done((f32[4096,512]{0,1:T(8,128)}, f32[4096,512]{0,1:T(8,128)S(1)}, u32[]{:S(2)}) %copy-start) | copy-done | bytes 8388632
  90.8 1.3 exponential_reduce_fusion
  92.1 0.5 broadcast_in_dim.2
  92.6 36.4 %all_to_all.19 = f32[32,2,4096]{2,1,0:T(2,128)S(1)} all-to-all(f32[32,2,4096]{2,1,0:T(2,128)S(1)} %broadcast_in_dim.2), channel_id=1, replica_groups=mesh['blk'=32,'own'=8] {'blk'}, dimensions={0} | all-to-all | bytes 2097152 | tf_op jit(solution)/shard_map/all_to_all | solution.py:12
  129.0 0.8 fusion.7
  129.8 0.6 copy_bitcast_fusion
  130.4 0.1 slice.71
  130.6 0.1 slice.72
  130.8 0.1 slice.82
  130.9 0.1 slice.83
  131.2 0.1 slice.73
  131.3 0.1 slice.74
  131.4 0.1 slice.84
  131.5 0.1 slice.85
  131.7 0.1 slice.75
  132.2 0.1 slice.77
  132.3 0.1 slice.78
  132.4 0.1 slice.88
  132.5 0.1 slice.89
  132.8 4.6 %fusion = f32[512]{0:T(512)S(1)} fusion(f32[4096,512]{0,1:T(8,128)} %copy-done, f32[4096]{0:T(1024)S(1)} %bitcast.15), kind=kLoop, calls=%fused_computation.3 | loop fusion | flops 4193792 | bytes 8407040 | tf_op jit(solution)/shard_map/reduce_sum | solution.py:104
  137.4 0.7 all_to_all.14
  138.1 6.4 %all-to-all-start.2 = ((f32[8,1,64]{2,1,0:T(1,128)}), f32[8,1,64]{2,1,0:T(1,128)S(1)}, u32[]{:S(2)}, u32[]{:S(2)}) async-start(f32[8,1,64]{2,1,0:T(1,128)} %all_to_all.14), calls=%async_computation.2 | async-start | bytes 8192 | tf_op jit(solution)/shard_map/all_to_all | solution.py:53
  144.5 9.9 %fusion.2 = f32[512,768]{1,0:T(8,128)} fusion(bf16[4096,768]{1,0:T(8,128)(2,1)} %all-gather.2.cloned.1.call-done, f32[4096,512]{0,1:T(8,128)} %copy-done, f32[4096]{0:T(1024)S(1)} %bitcast.16), kind=kOutput, calls=%fused_computation.5 | convolution fusion | flops 3225419776 | bytes 16269312 | tf_op jit(solution)/shard_map/dot_general | solution.py:98
  154.4 7.2 %all-to-all-start.1 = ((f32[8,64,768]{2,1,0:T(8,128)}), f32[8,64,768]{2,1,0:T(8,128)S(1)}, u32[]{:S(2)}, u32[]{:S(2)}) async-start(f32[8,64,768]{2,1,0:T(8,128)} %bitcast.14), calls=%async_computation.1 | async-start | bytes 3145728 | tf_op jit(solution)/shard_map/all_to_all | solution.py:53
  161.6 1.3 convert_element_type.6
  162.8 0.5 dynamic-slice_bitcast_fusion
  163.4 19.7 %all-to-all-done.1 = f32[8,64,768]{2,1,0:T(8,128)S(1)} async-done(((f32[8,64,768]{2,1,0:T(8,128)}), f32[8,64,768]{2,1,0:T(8,128)S(1)}, u32[]{:S(2)}, u32[]{:S(2)}) %all-to-all-start.1) | async-done | bytes 1572896 | tf_op jit(solution)/shard_map/all_to_all | solution.py:53
  183.2 1.7 add_divide_fusion
  (20 shorter events, 0.9 us)
Async XLA Ops:
  7.2 74.5 %all-gather.2.cloned.1.call-start = ((), (), s32[]{:S(2)}) async-start(), calls=%async_computation.3 | async-start | bytes 6488064 | tf_op jit(solution)/shard_map/all_gather | solution.py:95
  87.5 3.2 %copy-start = (f32[4096,512]{0,1:T(8,128)}, f32[4096,512]{0,1:T(8,128)S(1)}, u32[]{:S(2)}) copy-start(f32[4096,512]{0,1:T(8,128)S(1)} %get-tuple-element.14) | copy-start | bytes 25165828
  138.1 16.3 %all-to-all-start.2 = ((f32[8,1,64]{2,1,0:T(1,128)}), f32[8,1,64]{2,1,0:T(1,128)S(1)}, u32[]{:S(2)}, u32[]{:S(2)}) async-start(f32[8,1,64]{2,1,0:T(1,128)} %all_to_all.14), calls=%async_computation.2 | async-start | bytes 8192 | tf_op jit(solution)/shard_map/all_to_all | solution.py:53
  144.5 17.1 %copy-start.1 = (bf16[512,768]{1,0:T(8,128)(2,1)S(1)}, bf16[512,768]{1,0:T(8,128)(2,1)}, u32[]{:S(2)}) copy-start(bf16[512,768]{1,0:T(8,128)(2,1)} %param.4) | copy-start | bytes 2359300
  154.4 28.7 %all-to-all-start.1 = ((f32[8,64,768]{2,1,0:T(8,128)}), f32[8,64,768]{2,1,0:T(8,128)S(1)}, u32[]{:S(2)}, u32[]{:S(2)}) async-start(f32[8,64,768]{2,1,0:T(8,128)} %bitcast.14), calls=%async_computation.1 | async-start | bytes 3145728 | tf_op jit(solution)/shard_map/all_to_all | solution.py:53
  163.4 21.5 %copy-start.2 = (f32[64]{0:T(128)}, f32[64]{0:T(128)S(1)}, u32[]{:S(2)}) copy-start(f32[64]{0:T(128)S(1)} %reduce_sum.49) | copy-start | bytes 772
Sparse Core Ops, SparseCore 0:
  9.9 71.7 all-gather.1
where the time goes:
time: 192 us
  waiting for transfers between devices  92.8 us (48%)
  blocking collectives  36.4 us (19%)
  matrix products  15.8 us (8%)
  between operations  14.3 us (7%)
  starting transfers between devices  13.7 us (7%)
  other arithmetic  10.7 us (6%)
  local copies, waits for them, and re-layouts  8.15 us (4%)
    all_gather x1, waiting for transfers between devices, local(): row_block = lax.all_gather(embeddings, 'blk', axis=0, tiled=True)  72.4 us
    all_to_all x1, blocking collectives, copy_for_each(): return lax.all_to_all(copies, axis, split_axis=0, concat_axis=0, tiled=True)  36.4 us
    all_to_all x2, waiting for transfers between devices, sent_and_summed(): tiles = lax.all_to_all(cut_along(array, dim, count), axis, 0, 0, tiled=True)  19.7 us
    all_to_all x2, starting transfers between devices, sent_and_summed(): tiles = lax.all_to_all(cut_along(array, dim, count), axis, 0, 0, tiled=True)  13.6 us
    dot_general x1, matrix products, local(): lax.dot_general(resp_vals.astype(jnp.bfloat16), row_block, (((0,), (0,)),...  9.89 us
    dot_general x1, matrix products, score_rows(): lax.dot_general(row_block, centroids, (((1,), (1,)), ((), ())), preferred...  5.87 us
    reduce_sum x1, other arithmetic, local(): contrib, count_part = (contrib, jnp.sum(resp_vals, axis=0))  4.57 us
  transfers between devices with their start and end apart: 3, of which 2 were waited for; matrix products, arithmetic and copies ran while one was open for 7% of the time, Pallas kernels for 0%

commit v1 on v0

--- a/solution.py
+++ b/solution.py
@@ -5,6 +5,11 @@
 from jax.sharding import PartitionSpec as P
 
 prior_mass = 1.0
+
+
+def exchange_gather(x, axis, dim):
+    repeated = jnp.stack([x] * lax.axis_size(axis))
+    return jnp.concatenate(lax.all_to_all(repeated, axis, 0, 0), axis=dim)
 
 
 def copy_for_each(array, axis):
@@ -92,7 +97,7 @@
     log_total = peak_val + jnp.log(mass_sum)
     empty_sums = jnp.zeros((local_count, feat_dim), jnp.float32)
     empty_counts = jnp.zeros((local_count,), jnp.float32)
-    row_block = lax.all_gather(embeddings, "blk", axis=0, tiled=True)
+    row_block = exchange_gather(embeddings, "blk", 0)
     logits = score_rows(row_block, centroids, half_sq, log_weight, scale_root)
     resp_vals = jnp.exp(logits - log_total[:, None])
     contrib = lax.dot_general(

time: 192 us -> 338 us (1.76); the launches traced: 192 us -> 334 us
  waiting for transfers between devices: 92.8 us -> 226 us
  matrix products: 15.8 us -> 22.6 us
  starting transfers between devices: 13.7 us -> 18.3 us
  other arithmetic: 10.7 us -> 7.24 us
    all_to_all x0 -> x1, waiting for transfers between devices: none -> 134 us  [exchange_gather(): return jnp.concatenate(lax.all_to_all(repeated, axis, 0, 0), axis=dim)]
    dot_general x1 -> x2, matrix products: 5.87 us -> 14 us  [score_rows(): lax.dot_general(row_block, centroids, (((1,), (1,)), ((), ())), preferred...]
    all_to_all x0 -> x1, starting transfers between devices: none -> 4.69 us  [exchange_gather(): return jnp.concatenate(lax.all_to_all(repeated, axis, 0, 0), axis=dim)]
    reduce_sum x1 -> x0, other arithmetic: 4.57 us -> none  [local(): contrib, count_part = (contrib, jnp.sum(resp_vals, axis=0))]
  transfers between devices with their start and end apart: 3 -> 4, of which waited for: 2 -> 3; matrix products, arithmetic and copies ran while one was open for 7% -> 5% of each run, Pallas kernels for 0% -> 0%
where the time goes in v1:
time: 338 us; the launch traced here: 334 us
  waiting for transfers between devices  226 us (67%)
  blocking collectives  36.4 us (11%)
  matrix products  22.6 us (7%)
  starting transfers between devices  18.3 us (5%)
  between operations  14.3 us (4%)
  local copies, waits for them, and re-layouts  8.67 us (3%)
  other arithmetic  7.24 us (2%)
    all_to_all x1, waiting for transfers between devices, exchange_gather(): return jnp.concatenate(lax.all_to_all(repeated, axis, 0, 0), axis=dim)  134 us
    all_gather x1, waiting for transfers between devices, local(): lax.all_gather(embeddings, 'blk', axis=0, tiled=True)  72.4 us
    all_to_all x1, blocking collectives, copy_for_each(): return lax.all_to_all(copies, axis, split_axis=0, concat_axis=0, tiled=True)  36.4 us
    all_to_all x2, waiting for transfers between devices, sent_and_summed(): tiles = lax.all_to_all(cut_along(array, dim, count), axis, 0, 0, tiled=True)  19.1 us
    dot_general x2, matrix products, score_rows(): lax.dot_general(row_block, centroids, (((1,), (1,)), ((), ())), preferred...  14 us
    all_to_all x2, starting transfers between devices, sent_and_summed(): tiles = lax.all_to_all(cut_along(array, dim, count), axis, 0, 0, tiled=True)  13.6 us
    dot_general x1, matrix products, local(): lax.dot_general(resp_vals.astype(jnp.bfloat16), row_block, (((0,), (0,)),...  8.61 us
  transfers between devices with their start and end apart: 4, of which 3 were waited for; matrix products, arithmetic and copies ran while one was open for 5% of the time, Pallas kernels for 0%

profile of v1, /device:TPU:32, one launch (start us, length us, event | category | flops | bytes accessed | tf_op | source)
XLA Modules:
  0.0 333.6 jit_solution(16135556141622881189)
XLA Ops:
  7.2 0.7 all-gather.2.cloned.1.call-update
  7.9 1.4 multiply_reduce_fusion
  9.3 72.4 %all-gather.2.cloned.1.call-done = bf16[4096,768]{1,0:T(8,128)(2,1)} async-done(((bf16[128,768]{1,0:T(8,128)(2,1)}), bf16[4096,768]{1,0:T(8,128)(2,1)}) %all-gather.2.cloned.1.call-update) | async-done | bytes 6291472 | tf_op jit(solution)/shard_map/all_gather | solution.py:76
  81.6 5.8 %fusion = (f32[4096]{0:T(1024)S(1)}, f32[4096,512]{0,1:T(8,128)S(1)}) fusion(f32[512]{0:T(512)} %param.5, f32[512]{0:T(512)S(1)} %broadcast_multiply_fusion, bf16[4096,768]{1,0:T(8,128)(2,1)} %all-gather.2.cloned.1.call-done, bf16[512,768]{1,0:T(8,128)(2,1)} %param.4), kind=kOutput, calls=%fused_computation.3 | convolution fusion | flops 3229609984 | bytes 15486976 | tf_op jit(solution)/shard_map/dot_general | solution.py:63
  87.5 2.4 exponential_reduce_fusion
  90.0 0.5 broadcast_in_dim.2
  90.4 36.4 %all_to_all.24 = f32[32,2,4096]{2,1,0:T(2,128)S(1)} all-to-all(f32[32,2,4096]{2,1,0:T(2,128)S(1)} %broadcast_in_dim.2), channel_id=1, replica_groups=mesh['blk'=32,'own'=8] {'blk'}, dimensions={0} | all-to-all | bytes 2097152 | tf_op jit(solution)/shard_map/all_to_all | solution.py:17
  126.9 3.4 %stack.2 = bf16[32,128,768]{2,1,0:T(8,128)(2,1)} broadcast(bf16[128,768]{1,0:T(8,128)(2,1)S(1)} %copy-done.1), dimensions={1,2} | broadcast | bytes 6488064 | tf_op jit(solution)/shard_map/stack | solution.py:11
  130.2 4.7 %all-to-all-start = ((bf16[32,128,768]{2,1,0:T(8,128)(2,1)}), bf16[32,128,768]{2,1,0:T(8,128)(2,1)}, u32[]{:S(2)}, u32[]{:S(2)}) async-start(bf16[32,128,768]{2,1,0:T(8,128)(2,1)} %stack.2), calls=%async_computation | async-start | bytes 12582912 | tf_op jit(solution)/shard_map/all_to_all | solution.py:12
  134.9 1.2 fusion.4
  136.1 0.6 copy_bitcast_fusion
  136.7 0.1 slice.71
  136.9 0.1 slice.72
  137.0 0.1 slice.82
  137.2 0.1 slice.83
  137.7 0.1 slice.84
  137.8 0.1 slice.85
  138.0 0.1 slice.75
  138.5 0.1 slice.77
  138.6 0.1 slice.78
  138.7 0.1 slice.88
  138.8 0.1 slice.89
  139.1 133.8 %all-to-all-done = bf16[32,128,768]{2,1,0:T(8,128)(2,1)} async-done(((bf16[32,128,768]{2,1,0:T(8,128)(2,1)}), bf16[32,128,768]{2,1,0:T(8,128)(2,1)}, u32[]{:S(2)}, u32[]{:S(2)}) %all-to-all-start) | async-done | bytes 6291488 | tf_op jit(solution)/shard_map/all_to_all | solution.py:12
  272.9 8.1 %fusion.3 = (f32[512]{0:T(512)S(1)}, bf16[4096,512]{0,1:T(8,128)(2,1)}) fusion(f32[4096]{0:T(1024)S(1)} %bitcast.24, f32[512]{0:T(512)S(1)} %copy-done.2, f32[512]{0:T(512)S(1)} %broadcast_multiply_fusion, bf16[4096,768]{1,0:T(8,128)(2,1)} %bitcast, bf16[512,768]{1,0:T(8,128)(2,1)S(1)} %copy-done), kind=kOutput, calls=%fused_computation.22 | convolution fusion | flops 3233807872 | bytes 11294720 | tf_op jit(solution)/shard_map/dot_general | solution.py:63
  281.0 0.7 all_to_all.18
  281.7 6.4 %all-to-all-start.3 = ((f32[8,1,64]{2,1,0:T(1,128)}), f32[8,1,64]{2,1,0:T(1,128)S(1)}, u32[]{:S(2)}, u32[]{:S(2)}) async-start(f32[8,1,64]{2,1,0:T(1,128)} %all_to_all.18), calls=%async_computation.3 | async-start | bytes 8192 | tf_op jit(solution)/shard_map/all_to_all | solution.py:58
  288.1 8.6 %fusion.5 = f32[8,64,768]{2,1,0:T(8,128)} fusion(bf16[8,64,4096]{2,1,0:T(8,128)(2,1)} %bitcast.26, bf16[4096,768,1]{1,0,2:T(8,128)(2,1)} %bitcast.7), kind=kOutput, calls=%fused_computation.24 | convolution fusion | flops 3221225472 | bytes 12058624 | tf_op jit(solution)/shard_map/dot_general | solution.py:103
  296.7 7.2 %all-to-all-start.2 = ((f32[8,64,768]{2,1,0:T(8,128)}), f32[8,64,768]{2,1,0:T(8,128)S(1)}, u32[]{:S(2)}, u32[]{:S(2)}) async-start(f32[8,64,768]{2,1,0:T(8,128)} %fusion.5), calls=%async_computation.2 | async-start | bytes 3145728 | tf_op jit(solution)/shard_map/all_to_all | solution.py:58
  304.0 1.3 convert_element_type.7
  305.2 0.5 dynamic-slice_bitcast_fusion
  305.8 19.1 %all-to-all-done.2 = f32[8,64,768]{2,1,0:T(8,128)S(1)} async-done(((f32[8,64,768]{2,1,0:T(8,128)}), f32[8,64,768]{2,1,0:T(8,128)S(1)}, u32[]{:S(2)}, u32[]{:S(2)}) %all-to-all-start.2) | async-done | bytes 1572896 | tf_op jit(solution)/shard_map/all_to_all | solution.py:58
  325.0 1.7 add_divide_fusion
  (25 shorter events, 1.1 us)
Async XLA Ops:
  7.2 74.5 %all-gather.2.cloned.1.call-start = ((), (), s32[]{:S(2)}) async-start(), calls=%async_computation.4 | async-start | bytes 6488064 | tf_op jit(solution)/shard_map/all_gather | solution.py:76
  9.3 78.2 %copy-start.2 = (f32[512]{0:T(512)S(1)}, f32[512]{0:T(512)}, u32[]{:S(2)}) copy-start(f32[512]{0:T(512)} %param.5) | copy-start | bytes 6148
  87.5 39.4 %copy-start.1 = (bf16[128,768]{1,0:T(8,128)(2,1)S(1)}, bf16[128,768]{1,0:T(8,128)(2,1)}, u32[]{:S(2)}) copy-start(bf16[128,768]{1,0:T(8,128)(2,1)} %param.3) | copy-start | bytes 589828
  130.2 142.7 %all-to-all-start = ((bf16[32,128,768]{2,1,0:T(8,128)(2,1)}), bf16[32,128,768]{2,1,0:T(8,128)(2,1)}, u32[]{:S(2)}, u32[]{:S(2)}) async-start(bf16[32,128,768]{2,1,0:T(8,128)(2,1)} %stack.2), calls=%async_computation | async-start | bytes 12582912 | tf_op jit(solution)/shard_map/all_to_all | solution.py:12
  134.9 138.0 %copy-start = (bf16[512,768]{1,0:T(8,128)(2,1)S(1)}, bf16[512,768]{1,0:T(8,128)(2,1)}, u32[]{:S(2)}) copy-start(bf16[512,768]{1,0:T(8,128)(2,1)} %param.4) | copy-start | bytes 2359300
  281.7 15.0 %all-to-all-start.3 = ((f32[8,1,64]{2,1,0:T(1,128)}), f32[8,1,64]{2,1,0:T(1,128)S(1)}, u32[]{:S(2)}, u32[]{:S(2)}) async-start(f32[8,1,64]{2,1,0:T(1,128)} %all_to_all.18), calls=%async_computation.3 | async-start | bytes 8192 | tf_op jit(solution)/shard_map/all_to_all | solution.py:58
  296.7 28.2 %all-to-all-start.2 = ((f32[8,64,768]{2,1,0:T(8,128)}), f32[8,64,768]{2,1,0:T(8,128)S(1)}, u32[]{:S(2)}, u32[]{:S(2)}) async-start(f32[8,64,768]{2,1,0:T(8,128)} %fusion.5), calls=%async_computation.2 | async-start | bytes 3145728 | tf_op jit(solution)/shard_map/all_to_all | solution.py:58
  305.8 21.0 %copy-start.3 = (f32[64]{0:T(128)}, f32[64]{0:T(128)S(1)}, u32[]{:S(2)}) copy-start(f32[64]{0:T(128)S(1)} %reduce_sum.49) | copy-start | bytes 772
Sparse Core Ops, SparseCore 0:
  9.9 71.7 all-gather.1
